TPU v7x, 256 devices: a whole 4x4x8 slice. The times are simulated.
256 devices in a mesh: stn: 2 (over core), tm: 32 (over x, z_hi, y), ct: 4 (over z_lo).
Axes of the slice: x: 4, y: 4, z: 8 (z_hi: 2, z_lo: 4; z = z_hi * 4 + z_lo), core: 2. Of those that a mesh axis runs over, the one named last changes fastest.
Arguments:
- voltages: bfloat16 [2, 64, 2097152], P(None, ('stn', 'ct'), 'tm'), may hold values from -128 to 127, as said below
- delays: int32 [64], P(('stn', 'ct')), may hold values from 0 to 4095
Outputs:
- visibilities: float32 [2, 4096, 64, 64], P(None, ('tm', 'ct'), 'stn')
Inputs may be any that keep to these rules, and one draw needn't show every extreme that they name: `voltages`: every entry is a whole number.
All inputs are finite; a program needn't handle non-finite values.
Results may differ from a plain program's by a relative error of at most 0.0037.
Values may be sent and summed in bfloat16 or wider, within the bound.
A program may use at most 128 MiB of HBM per device.

v0:
```python
import math
import jax
import jax.numpy as jnp
from jax import lax
from jax.sharding import PartitionSpec as P

CHANNELS = 4096
RADIX = 64
TAPS = 16


def passed_along(block, axis, distance):
    devices = range(lax.axis_size(axis))
    route = [(i - distance, i) for i in devices if i - distance in devices]
    return lax.ppermute(block, axis, route)


def filter_table():
    length = TAPS * CHANNELS
    index = jnp.arange(length, dtype=jnp.int32).astype(jnp.float32)
    centred = (index - length / 2) / CHANNELS
    window = 0.5 - 0.5 * jnp.cos(2.0 * math.pi * index / length)
    factor = 1.0 / (48.0 * math.sqrt(CHANNELS))
    return (jnp.sinc(centred) * window * factor).reshape(TAPS, CHANNELS)


def dft_block(radix):
    steps = jnp.arange(radix, dtype=jnp.int32)
    grid = steps[:, None] * steps[None, :] % radix
    angle = 2.0 * math.pi * grid.astype(jnp.float32) / radix
    cosine = jnp.cos(angle)
    sine = jnp.sin(angle)
    upper = jnp.concatenate([cosine, sine], axis=1)
    lower = jnp.concatenate([-sine, cosine], axis=1)
    return jnp.concatenate([upper, lower], axis=0).astype(jnp.bfloat16)


def twiddles():
    second = CHANNELS // RADIX
    rows = jnp.arange(second, dtype=jnp.int32)
    cols = jnp.arange(RADIX, dtype=jnp.int32)
    grid = rows[:, None] * cols[None, :] % CHANNELS
    angle = 2.0 * math.pi * grid.astype(jnp.float32) / CHANNELS
    return (jnp.cos(angle), jnp.sin(angle))


def filtered(framed, table):
    count = framed.shape[-2] - TAPS + 1
    total = jnp.zeros(framed.shape[:-2] + (count, CHANNELS), jnp.float32)
    for tap in range(TAPS):
        begin = TAPS - 1 - tap
        total = total + table[tap] * framed[..., begin : begin + count, :].astype(jnp.float32)
    return total.astype(jnp.bfloat16)


def transform(branches):
    second = CHANNELS // RADIX
    number = branches.shape[0]
    stacked = branches.reshape(number, 2 * second, RADIX)
    inner = jnp.einsum(
        "kj,nja->nka", dft_block(second), stacked, preferred_element_type=jnp.float32
    )
    inner = inner.reshape(number, 2, second, RADIX)
    tw_cos, tw_sin = twiddles()
    real_part = inner[:, 0] * tw_cos + inner[:, 1] * tw_sin
    imag_part = inner[:, 1] * tw_cos - inner[:, 0] * tw_sin
    turned = (
        jnp.stack([real_part, imag_part], axis=2)
        .reshape(number, second, 2 * RADIX)
        .astype(jnp.bfloat16)
    )
    result = jnp.einsum("lj,nkj->nlk", dft_block(RADIX), turned, preferred_element_type=jnp.float32)
    return result.reshape(number, 2, CHANNELS).astype(jnp.bfloat16)


def pick_span(row, offset, span):
    return lax.dynamic_slice_in_dim(row, CHANNELS - offset, span, 1)


def on_device(voltages, delays):
    in_count = voltages.shape[1]
    frame_count = voltages.shape[2] // CHANNELS
    prior = passed_along(voltages, "tm", 1)
    extended = jnp.concatenate([prior, voltages], axis=2)
    span = (frame_count + TAPS - 1) * CHANNELS
    shifted = jax.vmap(
        lambda row, offset: pick_span(row, offset, span), in_axes=(1, 0), out_axes=1
    )(extended, delays)
    framed = shifted.reshape(2, in_count, frame_count + TAPS - 1, CHANNELS)
    branches = jnp.moveaxis(filtered(framed, filter_table()), 0, 2)
    spectra = transform(branches.reshape(in_count * frame_count, 2, CHANNELS))
    spectra = spectra.reshape(in_count, frame_count, 2, CHANNELS)
    moved = lax.all_to_all(
        lax.all_to_all(spectra, "tm", split_axis=3, concat_axis=1, tiled=True),
        "ct",
        split_axis=3,
        concat_axis=0,
        tiled=True,
    )
    local = moved.transpose(3, 2, 0, 1)
    total_frames = local.shape[3]
    swapped = jnp.stack([local[:, 1], -local[:, 0]], axis=1)
    left = jnp.stack([local, swapped], axis=0)
    summed = jnp.einsum(
        "ocjaf,cjbf->ocab",
        left,
        lax.all_gather(local, "stn", axis=2, tiled=True),
        preferred_element_type=jnp.float32,
    )
    return summed * (1.0 / total_frames)


def solution(mesh):
    return jax.shard_map(
        on_device,
        mesh=mesh,
        in_specs=(P(None, ("stn", "ct"), "tm"), P(("stn", "ct"))),
        out_specs=P(None, ("tm", "ct"), "stn", None),
        check_vma=False,
    )
```

profile of v0, /device:TPU:1, one launch (start us, length us, event | category | flops | bytes accessed | tf_op | source)
XLA Modules:
  0.0 411.2 jit_solution(17613483547774946661)
XLA Ops:
  6.5 3.8 copy.57
  10.3 5.4 %collective-permute-start = (bf16[2,8,65536]{2,0,1:T(2,128)(2,1)S(1)}, bf16[2,8,65536]{2,0,1:T(2,128)(2,1)}, u32[]{:S(2)}, u32[]{:S(2)}) collective-permute-start(bf16[2,8,65536]{2,0,1:T(2,128)(2,1)S(1)} %copy.57), channel_id=1, source_target_pairs={{0,4},{4,8},{8,12},{12,16},{16,20},{20,24},{24,28},{28,32},{32,36}... | collective-permute-start | bytes 6291464 | tf_op jit(solution)/shard_map/ppermute | solution.py:15
  17.4 41.2 %collective-permute-done = bf16[2,8,65536]{2,0,1:T(2,128)(2,1)} collective-permute-done((bf16[2,8,65536]{2,0,1:T(2,128)(2,1)S(1)}, bf16[2,8,65536]{2,0,1:T(2,128)(2,1)}, u32[]{:S(2)}, u32[]{:S(2)}) %collective-permute-start) | collective-permute-done | bytes 2097184 | tf_op jit(solution)/shard_map/ppermute | solution.py:15
  58.6 7.1 %maximum_bitcast_fusion = bf16[8,2,131072]{2,1,0:T(2,128)(2,1)} fusion(bf16[2,8,65536]{2,0,1:T(2,128)(2,1)S(1)} %copy.57, bf16[2,8,65536]{2,0,1:T(2,128)(2,1)} %collective-permute-done), kind=kLoop, calls=%fused_computation.2 | loop fusion | flops 8388608 | bytes 8388608 | tf_op jit(solution)/shard_map/vmap()/transpose | solution.py:77
  65.8 34.8 %while.1 = (s32[]{:T(128)}, bf16[8,2,131072]{2,1,0:T(2,128)(2,1)}, s32[8,3]{0,1:T(4,128)S(1)}, bf16[8,2,126976]{2,1,0:T(2,128)(2,1)}, s32[]{:T(128)}) while((s32[]{:T(128)}, bf16[8,2,131072]{2,1,0:T(2,128)(2,1)}, s32[8,3]{0,1:T(4,128)S(1)}, bf16[8,2,126976]{2,1,0:T(2,128)(2,1)}, s32[]{:T(128)}) %tuple.41), condition=%wide.while_cond, body=%wide.while_body.sunk | while | flops 2 | bytes 1016949 | solution.py:77
  75.1 3.7 dynamic-slice_dynamic-update-slice_fusion.2
  83.8 3.7 dynamic-slice_dynamic-update-slice_fusion.2
  96.8 3.7 dynamic-slice_dynamic-update-slice_fusion.2
  100.6 4.4 %copy.59 = bf16[8,2,126976]{2,0,1:T(8,128)(2,1)S(1)} copy(bf16[8,2,126976]{2,1,0:T(2,128)(2,1)} %get-tuple-element.12) | data formatting | bytes 8126464 | tf_op jit(solution)/shard_map/vmap()/gather | solution.py:77
  105.0 8.8 %fusion.5 = bf16[8,16,2,4096]{3,0,1,2:T(8,128)(2,1)S(1)} fusion(bf16[2,8,31,4096]{3,1,2,0:T(8,128)(2,1)S(1)} %bitcast.81, f32[4096]{0:T(1024)S(1)} %get-tuple-element.32, f32[4096]{0:T(1024)S(1)} %get-tuple-element.33, f32[4096]{0:T(1024)S(1)} %get-tuple-element.34, f32[4096]{0:T(1024)S(1)} %get-tuple-element.35, f32[4096]{0:T(1024)S(1)} %get-tuple-element.36, ...), kind=kLoop, calls=%fused_computation.16 | loop fusion | flops 50331648 | bytes 35913728 | tf_op jit(solution)/shard_map/transpose | solution.py:90
  116.0 4.2 %reshape_reshape.3 = bf16[128,128,64]{2,1,0:T(8,128)(2,1)} reshape(bf16[8,16,2,4096]{3,2,1,0:T(2,128)(2,1)S(1)} %copy.60) | data formatting | bytes 4194304 | tf_op jit(solution)/shard_map/reshape;reshape | solution.py:59
  120.1 4.8 %copy.61 = bf16[128,128,64]{1,0,2:T(8,128)(2,1)S(1)} copy(bf16[128,128,64]{2,1,0:T(8,128)(2,1)} %reshape_reshape.3) | data formatting | bytes 4194304 | tf_op jit(solution)/shard_map/reshape;reshape | solution.py:59
  126.3 5.0 %add_convert_fusion.1 = (bf16[128,64,1,64]{0,3,2,1:T(8,128)(2,1)S(1)}, bf16[128,64,1,64]{0,3,2,1:T(8,128)(2,1)S(1)}) fusion(f32[128,1,64,64]{0,2,1,3:T(8,128)S(1)} %get-tuple-element.26, f32[128,1,64,64]{0,2,1,3:T(8,128)S(1)} %get-tuple-element.25, f32[64,64]{1,0:T(8,128)S(1)} %get-tuple-element.49, f32[64,64]{1,0:T(8,128)S(1)} %get-tuple-element.50), kind=kLoop, calls=%fused_computation.15 | loop fusion | flops 4194304 | bytes 6324224 | tf_op jit(solution)/shard_map/convert
  132.3 3.9 copy.65
  136.2 6.7 %convert_element_type.154 = bf16[8,16,2,4096]{3,2,1,0:T(2,128)(2,1)S(1)} reshape(bf16[128,128,64]{2,1,0:T(8,128)(2,1)} %copy.65) | data formatting | bytes 4194304 | tf_op jit(solution)/shard_map/convert_element_type | solution.py:73
  142.9 16.7 %copy.66 = bf16[8,16,2,4096]{1,0,2,3:T(8,128)(2,1)} copy(bf16[8,16,2,4096]{3,2,1,0:T(2,128)(2,1)S(1)} %convert_element_type.154) | data formatting | bytes 4194304 | tf_op jit(solution)/shard_map/convert_element_type | solution.py:73
  159.6 19.7 %reshape.171 = bf16[32,2,16384]{2,1,0:T(2,128)(2,1)S(1)} reshape(bf16[4096,2,8,16]{3,2,1,0:T(8,128)(2,1)} %bitcast.82) | data formatting | bytes 4194304
  179.4 59.7 %all_to_all.36 = bf16[32,2,16384]{2,1,0:T(2,128)(2,1)} all-to-all(bf16[32,2,16384]{2,1,0:T(2,128)(2,1)S(1)} %reshape.171), channel_id=1, replica_groups=mesh['stn'=2,'tm'=32,'ct'=4] {'tm'}, dimensions={0} | all-to-all | bytes 4194304 | tf_op jit(solution)/shard_map/all_to_all | solution.py:94
  239.1 16.5 %reshape.172 = bf16[4096,2,8,16]{3,2,1,0:T(8,128)(2,1)} reshape(bf16[32,2,16384]{2,1,0:T(2,128)(2,1)} %all_to_all.36) | data formatting | bytes 4194304
  255.5 15.3 %copy.68 = bf16[8,32,16,2,128]{4,2,1,3,0:T(8,128)(2,1)S(1)} copy(bf16[8,32,16,2,128]{2,0,3,4,1:T(8,128)(2,1)} %bitcast.83) | data formatting | bytes 4194304 | tf_op jit(solution)/shard_map/all_to_all | solution.py:94
  270.8 4.0 copy.69
  274.8 104.3 %all_to_all.37 = bf16[8,512,2,128]{1,2,0,3:T(2,128)(2,1)S(1)} all-to-all(bf16[8,512,2,128]{1,2,0,3:T(2,128)(2,1)} %copy.69), channel_id=1, replica_groups=mesh['stn'=2,'tm'=32,'ct'=4] {'ct'}, dimensions={3} | all-to-all | bytes 4194304 | tf_op jit(solution)/shard_map/all_to_all | solution.py:93
  386.2 13.0 %all-gather.2.cloned.1.call-done = bf16[32,2,64,512]{3,2,1,0:T(8,128)(2,1)} async-done(((bf16[32,2,32,512]{3,2,1,0:T(8,128)(2,1)}), bf16[32,2,64,512]{3,2,1,0:T(8,128)(2,1)}) %all-gather.2.cloned.1.call-update) | async-done | bytes 4194320 | tf_op jit(solution)/shard_map/all_gather | solution.py:107
  399.1 4.1 fusion.16
  (46 shorter events, 37.9 us)
Async XLA Ops:
  6.5 9.2 %copy-start.1 = (s32[8]{0:T(128)S(1)}, s32[8]{0:T(128)}, u32[]{:S(2)}) copy-start(s32[8]{0:T(128)} %param.3) | copy-start | bytes 100
  6.5 392.6 %all-gather.2.cloned.1.call-start = ((), (), s32[]{:S(2)}) async-start(), calls=%async_computation.2 | async-start | bytes 6291456 | tf_op jit(solution)/shard_map/all_gather | solution.py:107
  10.3 48.3 %collective-permute-start = (bf16[2,8,65536]{2,0,1:T(2,128)(2,1)S(1)}, bf16[2,8,65536]{2,0,1:T(2,128)(2,1)}, u32[]{:S(2)}, u32[]{:S(2)}) collective-permute-start(bf16[2,8,65536]{2,0,1:T(2,128)(2,1)S(1)} %copy.57), channel_id=1, source_target_pairs={{0,4},{4,8},{8,12},{12,16},{16,20},{20,24},{24,28},{28,32},{32,36}... | collective-permute-start | bytes 6291464 | tf_op jit(solution)/shard_map/ppermute | solution.py:15
  382.8 16.4 %copy-start = (bf16[4,8,512,2,32]{2,1,0,3,4:T(8,128)(2,1)S(1)}, bf16[4,8,512,2,32]{2,1,0,3,4:T(8,128)(2,1)}, u32[]{:S(2)}) copy-start(bf16[4,8,512,2,32]{2,1,0,3,4:T(8,128)(2,1)} %copy.93) | copy-start | bytes 6291460
Sparse Core Ops, SparseCore 0:
  382.9 16.2 all-gather.1
where the time goes:
time: 413 us; the launch traced here: 411 us
  blocking collectives  164 us (40%)
  local copies, waits for them, and re-layouts  142 us (34%)
  waiting for transfers between devices  54.2 us (13%)
  other arithmetic  26.1 us (6%)
  between operations  13.5 us (3%)
  matrix products  5.65 us (1%)
  starting transfers between devices  5.4 us (1%)
    all_to_all x1, blocking collectives, on_device(): lax.all_to_all(lax.all_to_all(spectra, 'tm', split_axis=3, concat_axis=1,...  104 us
    all_to_all x1, blocking collectives, on_device(): lax.all_to_all(spectra, 'tm', split_axis=3, concat_axis=1, tiled=True)  59.7 us
    ppermute x1, waiting for transfers between devices, passed_along(): return lax.ppermute(block, axis, route)  41.2 us
    unnamed x8, local copies, waits for them, and re-layouts  39.9 us
    gather x24, local copies, waits for them, and re-layouts  34.8 us
    convert_element_type x3, local copies, waits for them, and re-layouts, transform(): return result.reshape(number, 2, CHANNELS).astype(jnp.bfloat16)  27.4 us
    all_to_all x2, local copies, waits for them, and re-layouts, on_device(): lax.all_to_all(spectra, 'tm', split_axis=3, concat_axis=1, tiled=True)  19.3 us
    all_gather x1, waiting for transfers between devices, on_device(): lax.all_gather(local, 'stn', axis=2, tiled=True)  13 us
  transfers between devices with their start and end apart: 2, of which 2 were waited for; matrix products, arithmetic and copies ran while one was open for 1% of the time, Pallas kernels for 0%

commit v1 on v0

--- a/solution.py
+++ b/solution.py
@@ -90,12 +90,20 @@
     branches = jnp.moveaxis(filtered(framed, filter_table()), 0, 2)
     spectra = transform(branches.reshape(in_count * frame_count, 2, CHANNELS))
     spectra = spectra.reshape(in_count, frame_count, 2, CHANNELS)
-    moved = lax.all_to_all(
-        lax.all_to_all(spectra, "tm", split_axis=3, concat_axis=1, tiled=True),
-        "ct",
-        split_axis=3,
-        concat_axis=0,
-        tiled=True,
+    moved = jnp.concatenate(
+        lax.all_to_all(
+            jnp.stack(
+                jnp.split(
+                    lax.all_to_all(spectra, "tm", split_axis=3, concat_axis=1, tiled=True),
+                    lax.axis_size("ct"),
+                    axis=3,
+                )
+            ),
+            "ct",
+            0,
+            0,
+        ),
+        axis=0,
     )
     local = moved.transpose(3, 2, 0, 1)
     total_frames = local.shape[3]

time: 413 us -> 423 us (1.024)
  local copies, waits for them, and re-layouts: 142 us -> 156 us
    another operation x0 -> x6, local copies, waits for them, and re-layouts: none -> 16.6 us  [the longest x5 12.3 us: on_device(): jnp.stack(jnp.split(lax.all_to_all(spectra, 'tm', split_axis=3, concat_ax...]
    all_to_all x2 -> x1, local copies, waits for them, and re-layouts: 19.3 us -> 15.3 us  [on_device(): lax.all_to_all(spectra, 'tm', split_axis=3, concat_axis=1, tiled=True)]
    unnamed x8 -> x14, local copies, waits for them, and re-layouts: 39.9 us -> 41.3 us
  transfers between devices with their start and end apart: 2 -> 2, of which waited for: 2 -> 2; matrix products, arithmetic and copies ran while one was open for 1% -> 2% of each run, Pallas kernels for 0% -> 0%
where the time goes in v1:
time: 423 us; the launch traced here: 421 us
  blocking collectives  164 us (39%)
  local copies, waits for them, and re-layouts  156 us (37%)
  waiting for transfers between devices  51.6 us (12%)
  other arithmetic  25.9 us (6%)
  between operations  13.6 us (3%)
  matrix products  5.65 us (1%)
  starting transfers between devices  5.4 us (1%)
    all_to_all x1, blocking collectives, on_device(): lax.all_to_all(jnp.stack(jnp.split(lax.all_to_all(spectra, 'tm', split_ax...  104 us
    all_to_all x1, blocking collectives, on_device(): lax.all_to_all(spectra, 'tm', split_axis=3, concat_axis=1, tiled=True)  59.7 us
    unnamed x14, local copies, waits for them, and re-layouts  41.3 us
    ppermute x1, waiting for transfers between devices, passed_along(): return lax.ppermute(block, axis, route)  41.2 us
    gather x24, local copies, waits for them, and re-layouts  35.3 us
    convert_element_type x3, local copies, waits for them, and re-layouts, transform(): return result.reshape(number, 2, CHANNELS).astype(jnp.bfloat16)  27.4 us
    all_to_all x1, local copies, waits for them, and re-layouts, on_device(): lax.all_to_all(spectra, 'tm', split_axis=3, concat_axis=1, tiled=True)  15.3 us
    another operation x5, local copies, waits for them, and re-layouts, on_device(): jnp.stack(jnp.split(lax.all_to_all(spectra, 'tm', split_axis=3, concat_ax...  12.3 us
  transfers between devices with their start and end apart: 2, of which 2 were waited for; matrix products, arithmetic and copies ran while one was open for 2% of the time, Pallas kernels for 0%

profile of v1, /device:TPU:1, one launch (start us, length us, event | category | flops | bytes accessed | tf_op | source)
XLA Modules:
  0.0 421.4 jit_solution(15673680900924384325)
XLA Ops:
  6.5 3.8 copy.47
  10.3 5.4 %collective-permute-start = (bf16[2,8,65536]{2,0,1:T(2,128)(2,1)S(1)}, bf16[2,8,65536]{2,0,1:T(2,128)(2,1)}, u32[]{:S(2)}, u32[]{:S(2)}) collective-permute-start(bf16[2,8,65536]{2,0,1:T(2,128)(2,1)S(1)} %copy.47), channel_id=1, source_target_pairs={{0,4},{4,8},{8,12},{12,16},{16,20},{20,24},{24,28},{28,32},{32,36}... | collective-permute-start | bytes 6291464 | tf_op jit(solution)/shard_map/ppermute | solution.py:15
  17.4 41.2 %collective-permute-done = bf16[2,8,65536]{2,0,1:T(2,128)(2,1)} collective-permute-done((bf16[2,8,65536]{2,0,1:T(2,128)(2,1)S(1)}, bf16[2,8,65536]{2,0,1:T(2,128)(2,1)}, u32[]{:S(2)}, u32[]{:S(2)}) %collective-permute-start) | collective-permute-done | bytes 2097184 | tf_op jit(solution)/shard_map/ppermute | solution.py:15
  58.6 7.1 %maximum_bitcast_fusion = bf16[8,2,131072]{2,1,0:T(2,128)(2,1)} fusion(bf16[2,8,65536]{2,0,1:T(2,128)(2,1)S(1)} %copy.47, bf16[2,8,65536]{2,0,1:T(2,128)(2,1)} %collective-permute-done), kind=kLoop, calls=%fused_computation.2 | loop fusion | flops 8388608 | bytes 8388608 | tf_op jit(solution)/shard_map/vmap()/transpose | solution.py:77
  65.8 35.3 %while.1 = (s32[]{:T(128)}, bf16[8,2,131072]{2,1,0:T(2,128)(2,1)}, s32[8,3]{0,1:T(4,128)S(1)}, bf16[8,2,126976]{2,1,0:T(2,128)(2,1)}, s32[]{:T(128)}) while((s32[]{:T(128)}, bf16[8,2,131072]{2,1,0:T(2,128)(2,1)}, s32[8,3]{0,1:T(4,128)S(1)}, bf16[8,2,126976]{2,1,0:T(2,128)(2,1)}, s32[]{:T(128)}) %tuple.42), condition=%wide.while_cond, body=%wide.while_body.sunk | while | flops 2 | bytes 1016949 | solution.py:77
  75.2 3.8 dynamic-slice_dynamic-update-slice_fusion.2
  97.3 3.8 dynamic-slice_dynamic-update-slice_fusion.2
  101.1 4.4 %copy.49 = bf16[8,2,126976]{2,0,1:T(8,128)(2,1)S(1)} copy(bf16[8,2,126976]{2,1,0:T(2,128)(2,1)} %get-tuple-element.12) | data formatting | bytes 8126464 | tf_op jit(solution)/shard_map/vmap()/gather | solution.py:77
  105.5 8.8 %fusion.5 = bf16[8,16,2,4096]{3,0,1,2:T(8,128)(2,1)S(1)} fusion(bf16[2,8,31,4096]{3,1,2,0:T(8,128)(2,1)S(1)} %bitcast.83, f32[4096]{0:T(1024)S(1)} %get-tuple-element.34, f32[4096]{0:T(1024)S(1)} %get-tuple-element.35, f32[4096]{0:T(1024)S(1)} %get-tuple-element.36, f32[4096]{0:T(1024)S(1)} %get-tuple-element.37, f32[4096]{0:T(1024)S(1)} %get-tuple-element.38, ...), kind=kLoop, calls=%fused_computation.22 | loop fusion | flops 50331648 | bytes 35913728 | tf_op jit(solution)/shard_map/transpose | solution.py:90
  116.5 4.2 reshape_reshape.3
  120.6 4.8 %copy.51 = bf16[128,128,64]{1,0,2:T(8,128)(2,1)S(1)} copy(bf16[128,128,64]{2,1,0:T(8,128)(2,1)} %reshape_reshape.3) | data formatting | bytes 4194304 | tf_op jit(solution)/shard_map/reshape;reshape | solution.py:59
  126.8 5.0 %add_convert_fusion.1 = (bf16[128,64,1,64]{0,3,2,1:T(8,128)(2,1)S(1)}, bf16[128,64,1,64]{0,3,2,1:T(8,128)(2,1)S(1)}) fusion(f32[128,1,64,64]{0,2,1,3:T(8,128)S(1)} %get-tuple-element.26, f32[128,1,64,64]{0,2,1,3:T(8,128)S(1)} %get-tuple-element.25, f32[64,64]{1,0:T(8,128)S(1)} %get-tuple-element.51, f32[64,64]{1,0:T(8,128)S(1)} %get-tuple-element.52), kind=kLoop, calls=%fused_computation.21 | loop fusion | flops 4194304 | bytes 6324224 | tf_op jit(solution)/shard_map/convert
  132.8 3.9 copy.55
  136.7 6.7 %convert_element_type.154 = bf16[8,16,2,4096]{3,2,1,0:T(2,128)(2,1)S(1)} reshape(bf16[128,128,64]{2,1,0:T(8,128)(2,1)} %copy.55) | data formatting | bytes 4194304 | tf_op jit(solution)/shard_map/convert_element_type | solution.py:73
  143.5 16.7 %copy.56 = bf16[8,16,2,4096]{1,0,2,3:T(8,128)(2,1)} copy(bf16[8,16,2,4096]{3,2,1,0:T(2,128)(2,1)S(1)} %convert_element_type.154) | data formatting | bytes 4194304 | tf_op jit(solution)/shard_map/convert_element_type | solution.py:73
  160.2 19.7 %reshape.175 = bf16[32,2,16384]{2,1,0:T(2,128)(2,1)S(1)} reshape(bf16[4096,2,8,16]{3,2,1,0:T(8,128)(2,1)} %bitcast.84) | data formatting | bytes 4194304
  179.9 59.7 %all_to_all.23 = bf16[32,2,16384]{2,1,0:T(2,128)(2,1)} all-to-all(bf16[32,2,16384]{2,1,0:T(2,128)(2,1)S(1)} %reshape.175), channel_id=1, replica_groups=mesh['stn'=2,'tm'=32,'ct'=4] {'tm'}, dimensions={0} | all-to-all | bytes 4194304 | tf_op jit(solution)/shard_map/all_to_all | solution.py:97
  239.6 16.5 %reshape.176 = bf16[4096,2,8,16]{3,2,1,0:T(8,128)(2,1)} reshape(bf16[32,2,16384]{2,1,0:T(2,128)(2,1)} %all_to_all.23) | data formatting | bytes 4194304
  256.1 15.3 %copy.58 = bf16[8,32,16,2,128]{4,2,1,3,0:T(8,128)(2,1)S(1)} copy(bf16[8,32,16,2,128]{2,0,3,4,1:T(8,128)(2,1)} %bitcast.85) | data formatting | bytes 4194304 | tf_op jit(solution)/shard_map/all_to_all | solution.py:97
  271.4 4.4 %slice_bitcast_fusion.3 = (bf16[1,8,512,2,32]{4,2,3,1,0:T(8,128)(2,1)}, bf16[1,8,512,2,32]{4,2,3,1,0:T(8,128)(2,1)}, bf16[1,8,512,2,32]{4,2,3,1,0:T(8,128)(2,1)}, bf16[1,8,512,2,32]{4,2,3,1,0:T(8,128)(2,1)}) fusion(bf16[8,512,2,128]{3,1,2,0:T(8,128)(2,1)S(1)} %bitcast.86), kind=kLoop, calls=%fused_computation.12 | loop fusion | bytes 4194304 | tf_op jit(solution)/shard_map/stack | solution.py:95
  285.1 104.1 %all_to_all.24 = bf16[4,8,512,2,32]{2,4,3,1,0:T(8,128)(2,1)S(1)} all-to-all(bf16[4,8,512,2,32]{2,4,3,1,0:T(8,128)(2,1)S(1)} %pad_maximum_fusion.1), channel_id=1, replica_groups=mesh['stn'=2,'tm'=32,'ct'=4] {'ct'}, dimensions={0} | all-to-all | bytes 4194304 | tf_op jit(solution)/shard_map/all_to_all | solution.py:94
  393.1 4.3 %copy.64 = bf16[1,32,2,32,512]{4,3,2,0,1:T(8,128)(2,1)} copy(bf16[1,32,2,32,512]{4,1,2,3,0:T(8,128)(2,1)} %bitcast.89) | data formatting | bytes 4194304 | tf_op jit(solution)/shard_map/stack | solution.py:111
  399.1 10.3 %all-gather.2.cloned.1.call-done = bf16[32,2,64,512]{3,2,1,0:T(8,128)(2,1)} async-done(((bf16[32,2,32,512]{3,2,1,0:T(8,128)(2,1)}), bf16[32,2,64,512]{3,2,1,0:T(8,128)(2,1)}) %all-gather.2.cloned.1.call-update) | async-done | bytes 4194320 | tf_op jit(solution)/shard_map/all_gather | solution.py:115
  409.4 4.1 fusion.16
  (57 shorter events, 49.9 us)
Async XLA Ops:
  6.5 9.2 %copy-start.4 = (s32[8]{0:T(128)S(1)}, s32[8]{0:T(128)}, u32[]{:S(2)}) copy-start(s32[8]{0:T(128)} %param.3) | copy-start | bytes 100
  6.5 402.9 %all-gather.2.cloned.1.call-start = ((), (), s32[]{:S(2)}) async-start(), calls=%async_computation.2 | async-start | bytes 6291456 | tf_op jit(solution)/shard_map/all_gather | solution.py:115
  10.3 48.3 %collective-permute-start = (bf16[2,8,65536]{2,0,1:T(2,128)(2,1)S(1)}, bf16[2,8,65536]{2,0,1:T(2,128)(2,1)}, u32[]{:S(2)}, u32[]{:S(2)}) collective-permute-start(bf16[2,8,65536]{2,0,1:T(2,128)(2,1)S(1)} %copy.47), channel_id=1, source_target_pairs={{0,4},{4,8},{8,12},{12,16},{16,20},{20,24},{24,28},{28,32},{32,36}... | collective-permute-start | bytes 6291464 | tf_op jit(solution)/shard_map/ppermute | solution.py:15
  275.7 6.5 %copy-start.2 = (bf16[1,8,512,2,32]{4,2,3,1,0:T(8,128)(2,1)S(1)}, bf16[1,8,512,2,32]{4,2,3,1,0:T(8,128)(2,1)}, u32[]{:S(2)}) copy-start(bf16[1,8,512,2,32]{4,2,3,1,0:T(8,128)(2,1)} %get-tuple-element.32) | copy-start | bytes 1572868
  389.2 1.4 copy-start.1
  393.1 4.3 %copy-start = (bf16[4,8,512,2,32]{2,1,0,3,4:T(8,128)(2,1)S(1)}, bf16[4,8,512,2,32]{2,1,0,3,4:T(8,128)(2,1)}, u32[]{:S(2)}) copy-start(bf16[4,8,512,2,32]{2,1,0,3,4:T(8,128)(2,1)} %copy.85) | copy-start | bytes 6291460
  397.5 11.9 %copy-start.3 = (bf16[1,32,2,32,512]{4,3,2,0,1:T(8,128)(2,1)S(1)}, bf16[1,32,2,32,512]{4,3,2,0,1:T(8,128)(2,1)}, u32[]{:S(2)}) copy-start(bf16[1,32,2,32,512]{4,3,2,0,1:T(8,128)(2,1)} %copy.64) | copy-start | bytes 6291460
Sparse Core Ops, SparseCore 0:
  393.2 16.1 all-gather.1
